TPU v7x, 256 devices: a whole 4x4x8 slice. The times are simulated.
256 devices in a mesh: acq: 16 (over y, x_lo, core), strip: 16 (over x_hi, z).
Axes of the slice: x: 4 (x_hi: 2, x_lo: 2; x = x_hi * 2 + x_lo), y: 4, z: 8, core: 2. Of those that a mesh axis runs over, the one named last changes fastest.
Arguments:
- raw_echoes: float32 [16, 2, 1024, 2048], P('acq', None, 'strip'), may hold values from -6 to 6
- range_filter: float32 [2, 2048], replicated, may hold values from -5 to 5
- azimuth_filter: float32 [2, 1024, 2048], P(None, None, 'strip'), may hold values from -5 to 5
- pair_mask: int32 [16, 2], P('acq'), may hold values 0 or 1
- inversion: float32 [16, 16, 2], P(None, 'acq'), may hold values from -1.5 to 1.5
Outputs:
- epoch_gradients: float32 [16, 2, 512, 256], P('acq', None, 'strip')
Inputs may be any that keep to these rules, and one draw needn't show every extreme that they name: `pair_mask`: 1 where the pair is in the network, 0 where it is not.
All inputs are finite; a program needn't handle non-finite values. No bound on the sum of `pair_mask` on one device may be relied on, other than what follows from the above.
Results may differ from a plain program's by a relative error of at most 0.00014.
Values sent between devices are 32-bit elements; how exact they have to be, the bound alone decides.
A program may use at most 64 MiB of HBM per device.

v0:
```python
import functools
import math

import jax
import jax.numpy as jnp
import numpy as np
from jax import lax
from jax.experimental import pallas as pl
from jax.experimental.pallas import tpu as pltpu
from jax.sharding import PartitionSpec as P

MESH = pl.DeviceIdType.MESH
EXACT = lax.Precision.HIGHEST
F32 = jnp.float32
LANES = 128
DEV = 16
Q = 64
CHUNKS = 4
WIDE = 32
PAIRS = [(1, j) for j in range(1, DEV)] + [(2, j) for j in range(2, DEV)]
ROWS = 8 * len(PAIRS)


def block_table(size, sign, scale=1.0):
    index = np.arange(size)
    angle = sign * 2.0 * math.pi / size * (index[:, None] * index[None, :] % size)
    cosine, sine = np.cos(angle) * scale, np.sin(angle) * scale
    return np.block([[cosine, sine], [-sine, cosine]])


def turn_table(count, width, size, sign):
    angle = sign * 2.0 * math.pi / size * (np.arange(count)[:, None] * np.arange(width)[None, :] % size)
    return np.cos(angle), np.sin(angle)


def sample_order():
    order = np.zeros(LANES, dtype=np.int64)
    for h in range(CHUNKS):
        for m in range(4):
            for k in range(8):
                order[WIDE * h + 8 * m + k] = WIDE * h + 4 * k + m
    return order


def tables():
    order = sample_order()
    w1 = block_table(128, -1.0)
    w2 = block_table(128, 1.0, 1.0 / 2048)
    w2 = w2[:, np.concatenate([order, 128 + order])]
    c1, s1 = turn_table(16, 128, 2048, -1.0)
    c2, s2 = turn_table(16, 128, 2048, 1.0)
    turn_range = np.concatenate([c1, s1, c2[:, order], s2[:, order]])
    w3 = block_table(64, -1.0)
    w4 = block_table(64, 1.0, 1.0 / 1024)
    c3, s3 = turn_table(16, 64, 1024, -1.0)
    c4, s4 = turn_table(16, 64, 1024, 1.0)
    turn_pulse = np.concatenate(
        [np.hstack([c3, c3]), np.hstack([-s3, s3]), np.hstack([c4, c4]), np.hstack([-s4, s4])]
    )
    pool = np.zeros((CHUNKS, 256, LANES))
    for h in range(CHUNKS):
        for q in range(Q):
            real, imag = 16 * h + q // 4, 64 + 16 * h + q // 4
            pool[h, q, real] = 0.25
            pool[h, 64 + q, real] = 0.25
            pool[h, 128 + q, imag] = -0.25
            pool[h, 192 + q, imag] = 0.25
    place = np.zeros((8, 32, 256))
    for m in range(8):
        for c in range(2):
            for k in range(16):
                place[m, 16 * c + k, 128 * c + 8 * k + m] = 1.0
    pick = np.zeros((LANES, LANES))
    pick[np.arange(LANES), order] = 1.0
    def split(w):
        high = np.asarray(w, np.float32).astype(jnp.bfloat16)
        return high, (w - high.astype(np.float64)).astype(np.float32).astype(jnp.bfloat16)

    def stacked(w):
        high, low = split(w)
        return np.concatenate([high, high, low])

    def squared(w):
        both = np.concatenate(split(w), axis=1)
        return np.concatenate([both, both])

    pool = np.concatenate([pool, pool], axis=1).reshape(-1, LANES).astype(jnp.bfloat16)
    single = [np.asarray(t, np.float32) for t in (turn_range, turn_pulse, place.reshape(-1, 256), pick, np.eye(LANES))]
    turn_range, turn_pulse, place, pick, eye = single
    return [stacked(w1), stacked(w2), turn_range, squared(w3), squared(w4), turn_pulse, pool, place, pick, eye]


def turned_quarter(re, im, sign):
    return (im, -re) if sign < 0 else (-im, re)


def dft4(x, sign):
    (r0, i0), (r1, i1), (r2, i2), (r3, i3) = x
    sr0, si0, dr0, di0 = r0 + r2, i0 + i2, r0 - r2, i0 - i2
    sr1, si1, dr1, di1 = r1 + r3, i1 + i3, r1 - r3, i1 - i3
    tr, ti = turned_quarter(dr1, di1, sign)
    return [(sr0 + sr1, si0 + si1), (dr0 + tr, di0 + ti), (sr0 - sr1, si0 - si1), (dr0 - tr, di0 - ti)]


def dft16(x, sign):
    stage = []
    for n2 in range(4):
        part = dft4([x[4 * n1 + n2] for n1 in range(4)], sign)
        moved = []
        for k1 in range(4):
            re, im = part[k1]
            if n2 * k1:
                angle = sign * 2.0 * math.pi * n2 * k1 / 16
                c, s = math.cos(angle), math.sin(angle)
                if n2 * k1 == 4:
                    re, im = turned_quarter(re, im, sign)
                else:
                    re, im = re * c - im * s, re * s + im * c
            moved.append((re, im))
        stage.append(moved)
    out = [None] * 16
    for k1 in range(4):
        last = dft4([stage[n2][k1] for n2 in range(4)], sign)
        for k2 in range(4):
            out[k1 + 4 * k2] = last[k2]
    return out


def swapped(v):
    return pltpu.roll(v, 64, 1)


def packed_dft4(x, unit):
    s0, d0, s1, d1 = x[0] + x[2], x[0] - x[2], x[1] + x[3], x[1] - x[3]
    t = swapped(d1) * unit
    return [s0 + s1, d0 + t, s0 - s1, d0 - t]


def packed_dft16(x, sign, unit):
    stage = []
    for n2 in range(4):
        part = packed_dft4([x[4 * n1 + n2] for n1 in range(4)], unit)
        moved = []
        for k1 in range(4):
            v = part[k1]
            if n2 * k1:
                angle = 2.0 * math.pi * n2 * k1 / 16
                c, s = math.cos(angle), math.sin(angle)
                v = swapped(v) * unit if n2 * k1 == 4 else v * c + swapped(v) * (unit * s)
            moved.append(v)
        stage.append(moved)
    out = [None] * 16
    for k1 in range(4):
        last = packed_dft4([stage[n2][k1] for n2 in range(4)], unit)
        for k2 in range(4):
            out[k1 + 4 * k2] = last[k2]
    return out


def halves(x):
    high = x.astype(jnp.bfloat16)
    return high, (x - high.astype(F32)).astype(jnp.bfloat16)


def dot(x, w, precision=None):
    return lax.dot_general(x, w, (((1,), (0,)), ((), ())), precision=precision, preferred_element_type=F32)


def dot_wide(x, w):
    high, low = halves(x)
    return dot(jnp.concatenate([high, low, high], axis=1), w)


def dot_square(x, w):
    y = dot(jnp.concatenate(halves(x), axis=1), w)
    return y[:, 0:128] + y[:, 128:256]


def dot_nt(x, w, precision=EXACT):
    return lax.dot_general(x, w, (((1,), (1,)), ((), ())), precision=precision, preferred_element_type=F32)


def kernel(
    raw, rfil, afil, inv, mask,
    w1_h, w2_h, tr_h, w3_h, w4_h, tp_h, pool_h, place_h, pick_h, eye_h,
    out,
    x, rf, af, iv, w1, w2, tr, w3, w4, tp, pool, place, pick, eye,
    spec, gain, turned, sent, got, mid, fcos, fsin, scene, stack, prod, look,
    wmine, wall, wide, side_s, side_r, low_s, low_r, slope, part_s, part_r,
    ld, ldx, s1, r1, s2, r2, s3, r3, s4, r4, s5, r5,
):
    a, s = lax.axis_index("acq"), lax.axis_index("strip")

    def load_x(g):
        rows = pl.ds(pl.multiple_of(8 * g, 8), 8)
        return pltpu.make_async_copy(raw.at[0, :, rows, :], x.at[:, rows, :], ldx.at[g])

    loads = [
        pltpu.make_async_copy(src, dst, ld.at[i])
        for i, (src, dst) in enumerate([
            (tr_h, tr), (rfil, rf), (inv, iv), (place_h, place), (eye_h, eye), (w1_h, w1), (w2_h, w2),
            (w3_h, w3), (w4_h, w4), (tp_h, tp), (pick_h, pick), (pool_h, pool), (afil, af),
        ])
    ]
    for copy in loads[:3]:
        copy.start()
    for g in range(8):
        load_x(g).start()
    for copy in loads[3:]:
        copy.start()

    barrier = pltpu.get_barrier_semaphore()

    def greet(i, _):
        pl.semaphore_signal(barrier, inc=1, device_id=(a, lax.rem(s + i, DEV)), device_id_type=MESH)
        pl.semaphore_signal(barrier, inc=1, device_id=(lax.rem(a + i, DEV), s), device_id_type=MESH)
        return 0

    lax.fori_loop(1, DEV, greet, 0)

    lane = lax.broadcasted_iota(jnp.int32, (8, LANES), 1)
    row8 = lax.broadcasted_iota(jnp.int32, (8, LANES), 0)
    half = jnp.where(lane < 64, -1.0, 1.0).astype(F32)

    loads[0].wait()
    loads[1].wait()
    loads[2].wait()
    usable = [jnp.where(a >= l + 1, mask[0, l].astype(F32), 0.0) for l in range(2)]
    wmine[...] = jnp.zeros((8, LANES), F32)
    for l in range(2):
        wmine[pl.ds(l, 1), pl.ds(0, DEV)] = iv[pl.ds(l, 1), :] * usable[l]

    def forward_range(g, _):
        load_x(g).wait()
        rows = pl.ds(pl.multiple_of(8 * g, 8), 8)
        field = [(x[0, rows, pl.ds(128 * n, 128)], x[1, rows, pl.ds(128 * n, 128)]) for n in range(16)]
        for k, (re, im) in enumerate(dft16(field, -1.0)):
            c, t = tr[pl.ds(k, 1), :], tr[pl.ds(16 + k, 1), :]
            at = pl.ds(pl.multiple_of(64 * k + 8 * g, 8), 8)
            spec[at, pl.ds(0, 128)] = re * c - im * t
            spec[at, pl.ds(128, 128)] = re * t + im * c
        return 0

    lax.fori_loop(0, 8, forward_range, 0)

    for copy in loads[3:5]:
        copy.wait()
    for c in range(2):
        for k in range(16):
            gain[pl.ds(16 * c + k, 1), pl.ds(0, 128)] = rf[pl.ds(c, 1), pl.ds(128 * k, 128)]
    across = dot_nt(eye[...], gain[:, pl.ds(0, 128)])
    ordered = dot(across[0:16, :], place[pl.ds(0, 32), :], EXACT)
    for m in range(1, 8):
        ordered = ordered + dot(across[16 * m : 16 * m + 16, :], place[pl.ds(32 * m, 32), :], EXACT)
    gain[pl.ds(0, 16), :] = ordered

    for copy in loads[5:7]:
        copy.wait()

    def filter_range(k, _):
        rows = pl.ds(pl.multiple_of(256 * k, 256), 256)
        z = dot_wide(spec[rows, :], w1[...])
        parts = []
        for i in range(4):
            g = gain[pl.ds(4 * k + i, 1), :]
            re, im = z[64 * i : 64 * i + 64, 0:128], z[64 * i : 64 * i + 64, 128:256]
            gr, gi = g[:, 0:128], g[:, 128:256]
            parts.append(jnp.concatenate([re * gr - im * gi, re * gi + im * gr], axis=1))
        y = dot_wide(jnp.concatenate(parts, axis=0), w2[...])
        for i in range(4):
            c, t = tr[pl.ds(32 + 4 * k + i, 1), :], tr[pl.ds(48 + 4 * k + i, 1), :]
            re, im = y[64 * i : 64 * i + 64, 0:128], y[64 * i : 64 * i + 64, 128:256]
            at = pl.ds(pl.multiple_of(256 * k + 64 * i, 64), 64)
            spec[at, pl.ds(0, 128)] = re * c - im * t
            spec[at, pl.ds(128, 128)] = re * t + im * c
        return 0

    lax.fori_loop(0, 4, filter_range, 0)

    def inverse_range(g, _):
        field = []
        for k in range(16):
            at = pl.ds(pl.multiple_of(64 * k + 8 * g, 8), 8)
            field.append((spec[at, pl.ds(0, 128)], spec[at, pl.ds(128, 128)]))
        for n, (re, im) in enumerate(dft16(field, 1.0)):
            turned[pl.ds(pl.multiple_of(128 * n + 8 * g, 8), 8), :] = re
            turned[pl.ds(pl.multiple_of(128 * n + 64 + 8 * g, 8), 8), :] = im
        return 0

    lax.fori_loop(0, 8, inverse_range, 0)

    pl.semaphore_wait(barrier, 2 * (DEV - 1))

    def strip_copy(h, i):
        p = lax.rem(s + i, DEV)
        return pltpu.make_async_remote_copy(
            src_ref=sent.at[pl.ds(pl.multiple_of(128 * p + WIDE * h, WIDE), WIDE), :],
            dst_ref=got.at[pl.ds(pl.multiple_of(128 * s + WIDE * h, WIDE), WIDE), :],
            send_sem=s1.at[h, i], recv_sem=r1.at[h, i], device_id=(a, p), device_id_type=MESH,
        )

    def acq_copy(h, i):
        p = lax.rem(a + i, DEV)
        return pltpu.make_async_remote_copy(
            src_ref=scene.at[pl.ds(pl.multiple_of(128 * p + WIDE * h, WIDE), WIDE), :],
            dst_ref=stack.at[pl.ds(pl.multiple_of(128 * a + WIDE * h, WIDE), WIDE), :],
            send_sem=s2.at[h, i], recv_sem=r2.at[h, i], device_id=(p, s), device_id_type=MESH,
        )

    def weight_copy(i):
        p = lax.rem(a + i, DEV)
        return pltpu.make_async_remote_copy(
            src_ref=wmine, dst_ref=wall.at[pl.ds(pl.multiple_of(8 * a, 8), 8), :],
            send_sem=s3.at[i], recv_sem=r3.at[i], device_id=(p, s), device_id_type=MESH,
        )

    def part_copy(i):
        p = lax.rem(a + i, DEV)
        return pltpu.make_async_remote_copy(
            src_ref=part_s.at[pl.ds(pl.multiple_of(8 * p, 8), 8), :],
            dst_ref=part_r.at[pl.ds(pl.multiple_of(8 * a, 8), 8), :],
            send_sem=s4.at[i], recv_sem=r4.at[i], device_id=(p, s), device_id_type=MESH,
        )

    def first_send(i, _):
        p = lax.rem(s + i, DEV)
        at = pl.ds(pl.multiple_of(128 * p, 128), 128)
        sent[at, :] = turned[at, :].T
        strip_copy(0, i).start()
        return 0

    lax.fori_loop(1, DEV, first_send, 0)
    for h in range(1, CHUNKS):
        lax.fori_loop(1, DEV, lambda i, _, h=h: (strip_copy(h, i).start(), 0)[1], 0)
    lax.fori_loop(1, DEV, lambda i, _: (weight_copy(i).start(), 0)[1], 0)
    own = pl.ds(pl.multiple_of(128 * s, 128), 128)
    got[own, :] = turned[own, :].T
    wall[pl.ds(pl.multiple_of(8 * a, 8), 8), :] = wmine[...]

    for copy in loads[7:]:
        copy.wait()

    def turn_filter(k, _):
        re, im = af[0, pl.ds(k, 64, stride=16), :], af[1, pl.ds(k, 64, stride=16), :]
        c = dot_nt(pick[...], jnp.concatenate([re, re], axis=0))
        t = dot_nt(pick[...], jnp.concatenate([-im, im], axis=0))
        for h in range(CHUNKS):
            at = pl.ds(pl.multiple_of(512 * h + WIDE * k, WIDE), WIDE)
            fcos[at, :] = c[WIDE * h : WIDE * h + WIDE, :]
            fsin[at, :] = t[WIDE * h : WIDE * h + WIDE, :]
        return 0

    lax.fori_loop(0, 16, turn_filter, 0)

    lax.fori_loop(1, DEV, lambda i, _: (weight_copy(i).wait_recv(), 0)[1], 0)
    for l in range(2):
        columns = wall[pl.ds(l, 16, stride=8), :]
        for e in range(DEV):
            wide[pl.ds(16 * (16 * l + e), 16), :] = jnp.broadcast_to(columns[:, e : e + 1], (16, LANES))

    def azimuth(h):
        def forward(m, _):
            field = [got[pl.ds(pl.multiple_of(128 * n + WIDE * h + 8 * m, 8), 8), :] for n in range(16)]
            for k, v in enumerate(packed_dft16(field, -1.0, -half)):
                v = v * tp[pl.ds(k, 1), :] + swapped(v) * tp[pl.ds(16 + k, 1), :]
                mid[pl.ds(pl.multiple_of(WIDE * k + 8 * m, 8), 8), :] = v
            return 0

        lax.fori_loop(0, 4, forward, 0)
        at = pl.ds(pl.multiple_of(512 * h, 512), 512)
        z = dot_square(mid[...], w3[...])
        z = z * fcos[at, :] + swapped(z) * fsin[at, :]
        z = dot_square(z, w4[...])
        z2 = swapped(z)
        for k in range(16):
            piece = slice(WIDE * k, WIDE * k + WIDE)
            mid[pl.ds(WIDE * k, WIDE), :] = (
                z[piece, :] * tp[pl.ds(32 + k, 1), :] + z2[piece, :] * tp[pl.ds(48 + k, 1), :]
            )

        def inverse(m, _):
            field = [mid[pl.ds(pl.multiple_of(WIDE * k + 8 * m, 8), 8), :] for k in range(16)]
            for n, v in enumerate(packed_dft16(field, 1.0, half)):
                scene[pl.ds(pl.multiple_of(128 * n + WIDE * h + 8 * m, 8), 8), :] = v
            return 0

        lax.fori_loop(0, 4, inverse, 0)

    def products(h):
        held = {}
        for j in range(DEV):
            held[j] = [stack[pl.ds(pl.multiple_of(128 * j + WIDE * h + 8 * m, 8), 8), :] for m in range(4)]
            later = [swapped(v) for v in held[j]]
            for l in (1, 2):
                if j >= l:
                    same, cross = 0.0, 0.0
                    for m in range(4):
                        same = same + held[j - l][m] * held[j][m]
                        cross = cross + held[j - l][m] * later[m]
                    p = PAIRS.index((l, j))
                    prod[pl.ds(8 * p, 8), pl.ds(0, 128)] = same
                    prod[pl.ds(8 * p, 8), pl.ds(128, 128)] = cross
        pooled = dot(jnp.concatenate(halves(prod[...]), axis=1), pool[pl.ds(pl.multiple_of(512 * h, 512), 512), :])

        @pl.when(h == 0)
        def _():
            look[...] = pooled

        @pl.when(h > 0)
        def _():
            look[...] += pooled

    def turn(h, _):
        @pl.when(h < CHUNKS)
        def _():
            lax.fori_loop(1, DEV, lambda i, _: (strip_copy(h, i).wait_recv(), 0)[1], 0)
            azimuth(h)
            lax.fori_loop(1, DEV, lambda i, _: (acq_copy(h, i).start(), 0)[1], 0)
            stack[pl.ds(pl.multiple_of(128 * a + WIDE * h, WIDE), WIDE), :] = scene[
                pl.ds(pl.multiple_of(128 * a + WIDE * h, WIDE), WIDE), :
            ]

        @pl.when(h > 0)
        def _():
            lax.fori_loop(1, DEV, lambda i, _: (acq_copy(h - 1, i).wait_recv(), 0)[1], 0)
            products(h - 1)

        return 0

    lax.fori_loop(0, CHUNKS + 1, turn, 0)

    side = [jnp.zeros((8, LANES), F32), jnp.zeros((8, LANES), F32)]
    for p in range(len(PAIRS)):
        v = look[pl.ds(8 * p, 8), :]
        v = pltpu.roll(v, p % 16, 1) if p % 16 else v
        side[p // 16] = jnp.where(lane % 16 == p % 16, v, side[p // 16])
    side_s[pl.ds(0, 8), :] = side[0]
    side_s[pl.ds(8, 8), :] = side[1]
    low_s[pl.ds(0, len(PAIRS)), :] = look[pl.ds(0, len(PAIRS), stride=8), :]
    side_copy = pltpu.make_async_remote_copy(
        src_ref=side_s, dst_ref=side_r, send_sem=s5.at[0], recv_sem=r5.at[0],
        device_id=(lax.rem(a + DEV - 1, DEV), s), device_id_type=MESH,
    )
    low_copy = pltpu.make_async_remote_copy(
        src_ref=low_s.at[pl.ds(0, len(PAIRS)), :], dst_ref=low_r.at[pl.ds(0, len(PAIRS)), :], send_sem=s5.at[1], recv_sem=r5.at[1],
        device_id=(a, lax.rem(s + DEV - 1, DEV)), device_id_type=MESH,
    )
    side_copy.start()
    low_copy.start()
    side_copy.wait_recv()
    low_copy.wait_recv()

    inner = a < DEV - 1
    above = s < DEV - 1
    border = [jnp.where(inner, side_r[pl.ds(8 * i, 8), :], 0.0) for i in range(2)]
    low_r[...] = jnp.where(above, pltpu.roll(low_r[...], 112, 1), 0.0)
    last_look = lane % 16 == 15
    corner = (row8 == 7) & (lane % 64 >= 48)
    for p in range(len(PAIRS)):
        v = look[pl.ds(8 * p, 8), :]
        after = pltpu.roll(v, 63, 1)
        edge = pltpu.roll(border[p // 16], (64 + 15 - p % 16) % 128, 1)
        after = jnp.where(last_look, edge, after)
        up = jnp.where(row8 == 0, pltpu.roll(v, 48, 1), pltpu.roll(v, 64, 1))
        up = pltpu.roll(up, 7, 0)
        up = jnp.where(corner, jnp.broadcast_to(low_r[pl.ds(p, 1), :], (8, LANES)), up)
        w = v * -half
        azim, rang = w * after, w * up
        slope[pl.ds(8 * p, 8), :] = jnp.where(lane < 64, azim, rang) + pltpu.roll(
            jnp.where(lane < 64, rang, azim), 64, 1
        )

    total = [None] * DEV
    for p, (l, j) in enumerate(PAIRS):
        v = slope[pl.ds(8 * p, 8), :]
        for e in range(DEV):
            term = wide[pl.ds(16 * (16 * (l - 1) + e) + j, 1), :] * v
            total[e] = term if total[e] is None else total[e] + term
    for e in range(DEV):
        part_s[pl.ds(8 * e, 8), :] = total[e]
    lax.fori_loop(1, DEV, lambda i, _: (part_copy(i).start(), 0)[1], 0)
    mine = pl.ds(pl.multiple_of(8 * a, 8), 8)
    part_r[mine, :] = part_s[mine, :]
    lax.fori_loop(1, DEV, lambda i, _: (part_copy(i).wait_recv(), 0)[1], 0)

    for d in range(2):
        for h in range(CHUNKS):
            for u in range(2):
                tile = None
                for t in range(8):
                    v = part_r[pl.ds(8 * (8 * u + t), 8), :]
                    shift = 16 * (t - 4 * d - h) % 128
                    v = pltpu.roll(v, shift, 1) if shift else v
                    tile = v if tile is None else jnp.where(lane // 16 == t, v, tile)
                out[0, d, pl.ds(8 * h, 8), pl.ds(128 * u, 128)] = tile

    for h in range(CHUNKS):
        lax.fori_loop(1, DEV, lambda i, _, h=h: (strip_copy(h, i).wait_send(), 0)[1], 0)
        lax.fori_loop(1, DEV, lambda i, _, h=h: (acq_copy(h, i).wait_send(), 0)[1], 0)
    lax.fori_loop(1, DEV, lambda i, _: (weight_copy(i).wait_send(), 0)[1], 0)
    lax.fori_loop(1, DEV, lambda i, _: (part_copy(i).wait_send(), 0)[1], 0)
    side_copy.wait_send()
    low_copy.wait_send()


def per_device(raw_echoes, range_filter, azimuth_filter, pair_mask, inversion):
    consts = tables()
    hbm = pl.BlockSpec(memory_space=pl.ANY)
    smem = pl.BlockSpec(memory_space=pltpu.SMEM)
    vmem = lambda *shape: pltpu.VMEM(shape, F32)
    dma = pltpu.SemaphoreType.DMA
    return pl.pallas_call(
        kernel,
        out_shape=jax.ShapeDtypeStruct((1, 2, WIDE, 256), F32),
        in_specs=[hbm, hbm, hbm, hbm, smem] + [hbm] * len(consts),
        out_specs=pl.BlockSpec(memory_space=pltpu.VMEM),
        scratch_shapes=[vmem(2, 64, 2048), vmem(2, 2048), vmem(2, 1024, 128), vmem(2, DEV)]
        + [pltpu.VMEM(c.shape, c.dtype) for c in consts]
        + [
            vmem(1024, 256), vmem(32, 256), vmem(2048, 128), vmem(2048, 128), vmem(2048, 128),
            vmem(512, 128), vmem(2048, 128), vmem(2048, 128), vmem(2048, 128), vmem(2048, 128),
            vmem(ROWS, 256), vmem(ROWS, 128),
            vmem(8, 128), vmem(128, 128), vmem(512, 128), vmem(16, 128), vmem(16, 128), vmem(32, 128), vmem(32, 128),
            vmem(ROWS, 128), vmem(128, 128), vmem(128, 128),
            dma((13,)), dma((8,)), dma((CHUNKS, DEV)), dma((CHUNKS, DEV)), dma((CHUNKS, DEV)), dma((CHUNKS, DEV)),
            dma((DEV,)), dma((DEV,)), dma((DEV,)), dma((DEV,)), dma((2,)), dma((2,)),
        ],
        compiler_params=pltpu.CompilerParams(collective_id=0, has_side_effects=True, vmem_limit_bytes=60 * 1024 * 1024),
    )(raw_echoes, range_filter, azimuth_filter, inversion[:, 0, :].T, pair_mask, *[jnp.asarray(c) for c in consts])


def solution(mesh):
    return jax.shard_map(
        per_device,
        mesh=mesh,
        in_specs=(
            P("acq", None, "strip", None),
            P(),
            P(None, None, "strip"),
            P("acq", None),
            P(None, "acq", None),
        ),
        out_specs=P("acq", None, "strip", None),
        check_vma=False,
    )
```

profile of v0, /device:TPU:1, one launch (start us, length us, event | category | flops | bytes accessed | tf_op | source)
XLA Modules:
  0.0 59.6 jit_solution(10793364642611766903)
XLA Ops:
  0.0 58.2 %shard_map.145 = f32[1,2,32,256]{3,2,1,0:T(8,128)} custom-call(f32[1,2,64,2048]{3,2,1,0:T(8,128)} %raw.1, f32[2,2048]{1,0:T(2,128)} %rfil.1, f32[2,1024,128]{2,1,0:T(8,128)} %afil.1, f32[2,16]{1,0:T(2,128)} %bitcast.3, s32[1,2]{1,0:T(1,128)} %mask.1, bf16[768,256]{1,0:T(8,128)(2,1)} %constant.20.clone.w1_h, bf16[768,256]{1,0:T(8,128)(2,1)} %constant.21.clone.w2_h, ...), custom_call_target="tpu_custom_call" | custom-call | tf_op jit(solution)/shard_map/pallas_call | solution.py:512
  58.2 1.5 %copy.17 = f32[1,2,32,256]{3,2,1,0:T(8,128)} copy(f32[1,2,32,256]{3,2,1,0:T(8,128)} %shard_map.145) | data formatting | bytes 131072
where the time goes:
time: 59.8 us; the launch traced here: 59.6 us
  Pallas kernels  58.2 us (97%)
  local copies, waits for them, and re-layouts  1.47 us (2%)
    pallas_call x1, Pallas kernels, per_device(): pl.pallas_call(kernel, out_shape=jax.ShapeDtypeStruct((1, 2, WIDE, 256),...  58.2 us
    unnamed x1, local copies, waits for them, and re-layouts  1.47 us

commit v1 on v0

--- a/solution.py
+++ b/solution.py
@@ -17,6 +17,10 @@
 Q = 64
 CHUNKS = 4
 WIDE = 32
+TILES = 16
+PAIR_UNITS = 7
+LAG = 3
+UNITS = [(2 * u, 2) for u in range(PAIR_UNITS)] + [(t, 1) for t in range(2 * PAIR_UNITS, TILES)]
 PAIRS = [(1, j) for j in range(1, DEV)] + [(2, j) for j in range(2, DEV)]
 ROWS = 8 * len(PAIRS)
 
@@ -65,11 +69,6 @@
             pool[h, 64 + q, real] = 0.25
             pool[h, 128 + q, imag] = -0.25
             pool[h, 192 + q, imag] = 0.25
-    place = np.zeros((8, 32, 256))
-    for m in range(8):
-        for c in range(2):
-            for k in range(16):
-                place[m, 16 * c + k, 128 * c + 8 * k + m] = 1.0
     pick = np.zeros((LANES, LANES))
     pick[np.arange(LANES), order] = 1.0
     def split(w):
@@ -85,9 +84,9 @@
         return np.concatenate([both, both])
 
     pool = np.concatenate([pool, pool], axis=1).reshape(-1, LANES).astype(jnp.bfloat16)
-    single = [np.asarray(t, np.float32) for t in (turn_range, turn_pulse, place.reshape(-1, 256), pick, np.eye(LANES))]
-    turn_range, turn_pulse, place, pick, eye = single
-    return [stacked(w1), stacked(w2), turn_range, squared(w3), squared(w4), turn_pulse, pool, place, pick, eye]
+    turn_range, turn_pulse = np.asarray(turn_range, np.float32), np.asarray(turn_pulse, np.float32)
+    pick = np.concatenate([pick, pick, pick], axis=1).astype(jnp.bfloat16)
+    return [stacked(w1), stacked(w2), turn_range, squared(w3), squared(w4), turn_pulse, pool, pick]
 
 
 def turned_quarter(re, im, sign):
@@ -182,14 +181,23 @@
 
 def kernel(
     raw, rfil, afil, inv, mask,
-    w1_h, w2_h, tr_h, w3_h, w4_h, tp_h, pool_h, place_h, pick_h, eye_h,
+    w1_h, w2_h, tr_h, w3_h, w4_h, tp_h, pool_h, pick_h,
     out,
-    x, rf, af, iv, w1, w2, tr, w3, w4, tp, pool, place, pick, eye,
+    x, rf, af, iv, w1, w2, tr, w3, w4, tp, pool, pick,
     spec, gain, turned, sent, got, mid, fcos, fsin, scene, stack, prod, look,
     wmine, wall, wide, side_s, side_r, low_s, low_r, slope, part_s, part_r,
-    ld, ldx, s1, r1, s2, r2, s3, r3, s4, r4, s5, r5,
+    ld, ldx, s1, r1, s2, r2, s3, r3,
 ):
     a, s = lax.axis_index("acq"), lax.axis_index("strip")
+
+    barrier = pltpu.get_barrier_semaphore()
+
+    def greet(i, _):
+        pl.semaphore_signal(barrier, inc=1, device_id=(a, lax.rem(s + i, DEV)), device_id_type=MESH)
+        pl.semaphore_signal(barrier, inc=1, device_id=(lax.rem(a + i, DEV), s), device_id_type=MESH)
+        return 0
+
+    lax.fori_loop(1, DEV, greet, 0, unroll=True)
 
     def load_x(g):
         rows = pl.ds(pl.multiple_of(8 * g, 8), 8)
@@ -198,8 +206,8 @@
     loads = [
         pltpu.make_async_copy(src, dst, ld.at[i])
         for i, (src, dst) in enumerate([
-            (tr_h, tr), (rfil, rf), (inv, iv), (place_h, place), (eye_h, eye), (w1_h, w1), (w2_h, w2),
-            (w3_h, w3), (w4_h, w4), (tp_h, tp), (pick_h, pick), (pool_h, pool), (afil, af),
+            (rfil, rf), (inv, iv), (tr_h, tr), (w1_h, w1), (w2_h, w2),
+            (pick_h, pick), (afil, af), (w3_h, w3), (w4_h, w4), (tp_h, tp), (pool_h, pool),
         ])
     ]
     for copy in loads[:3]:
@@ -209,26 +217,31 @@
     for copy in loads[3:]:
         copy.start()
 
-    barrier = pltpu.get_barrier_semaphore()
-
-    def greet(i, _):
-        pl.semaphore_signal(barrier, inc=1, device_id=(a, lax.rem(s + i, DEV)), device_id_type=MESH)
-        pl.semaphore_signal(barrier, inc=1, device_id=(lax.rem(a + i, DEV), s), device_id_type=MESH)
-        return 0
-
-    lax.fori_loop(1, DEV, greet, 0)
-
     lane = lax.broadcasted_iota(jnp.int32, (8, LANES), 1)
     row8 = lax.broadcasted_iota(jnp.int32, (8, LANES), 0)
     half = jnp.where(lane < 64, -1.0, 1.0).astype(F32)
 
     loads[0].wait()
     loads[1].wait()
-    loads[2].wait()
     usable = [jnp.where(a >= l + 1, mask[0, l].astype(F32), 0.0) for l in range(2)]
     wmine[...] = jnp.zeros((8, LANES), F32)
     for l in range(2):
         wmine[pl.ds(l, 1), pl.ds(0, DEV)] = iv[pl.ds(l, 1), :] * usable[l]
+
+    for c in range(2):
+        for k in range(16):
+            gain[pl.ds(16 * c + k, 1), pl.ds(0, 128)] = rf[pl.ds(c, 1), pl.ds(128 * k, 128)]
+    eye = (lax.broadcasted_iota(jnp.int32, (128, 128), 0) == lax.broadcasted_iota(jnp.int32, (128, 128), 1)).astype(F32)
+    across = dot_nt(eye, gain[:, pl.ds(0, 128)])
+    to = lax.broadcasted_iota(jnp.int32, (32, 256), 1)
+    meets = to // 8 == lax.broadcasted_iota(jnp.int32, (32, 256), 0)
+    ordered = None
+    for m in range(8):
+        place = jnp.where(meets & (to % 8 == m), 1.0, 0.0).astype(F32)
+        part = dot(across[16 * m : 16 * m + 16, :], place, EXACT)
+        ordered = part if ordered is None else ordered + part
+    gain[pl.ds(0, 16), :] = ordered
+    loads[2].wait()
 
     def forward_range(g, _):
         load_x(g).wait()
@@ -241,20 +254,9 @@
             spec[at, pl.ds(128, 128)] = re * t + im * c
         return 0
 
-    lax.fori_loop(0, 8, forward_range, 0)
+    lax.fori_loop(0, 8, forward_range, 0, unroll=2)
 
     for copy in loads[3:5]:
-        copy.wait()
-    for c in range(2):
-        for k in range(16):
-            gain[pl.ds(16 * c + k, 1), pl.ds(0, 128)] = rf[pl.ds(c, 1), pl.ds(128 * k, 128)]
-    across = dot_nt(eye[...], gain[:, pl.ds(0, 128)])
-    ordered = dot(across[0:16, :], place[pl.ds(0, 32), :], EXACT)
-    for m in range(1, 8):
-        ordered = ordered + dot(across[16 * m : 16 * m + 16, :], place[pl.ds(32 * m, 32), :], EXACT)
-    gain[pl.ds(0, 16), :] = ordered
-
-    for copy in loads[5:7]:
         copy.wait()
 
     def filter_range(k, _):
@@ -275,7 +277,7 @@
             spec[at, pl.ds(128, 128)] = re * t + im * c
         return 0
 
-    lax.fori_loop(0, 4, filter_range, 0)
+    lax.fori_loop(0, 4, filter_range, 0, unroll=True)
 
     def inverse_range(g, _):
         field = []
@@ -287,31 +289,30 @@
             turned[pl.ds(pl.multiple_of(128 * n + 64 + 8 * g, 8), 8), :] = im
         return 0
 
-    lax.fori_loop(0, 8, inverse_range, 0)
-
-    pl.semaphore_wait(barrier, 2 * (DEV - 1))
-
-    def strip_copy(h, i):
+    lax.fori_loop(0, 8, inverse_range, 0, unroll=2)
+
+    def rows_of(block, tile, count):
+        return pl.ds(pl.multiple_of(128 * block + 8 * tile, 8), 8 * count)
+
+    def strip_copy(u, tile, count, i):
         p = lax.rem(s + i, DEV)
         return pltpu.make_async_remote_copy(
-            src_ref=sent.at[pl.ds(pl.multiple_of(128 * p + WIDE * h, WIDE), WIDE), :],
-            dst_ref=got.at[pl.ds(pl.multiple_of(128 * s + WIDE * h, WIDE), WIDE), :],
-            send_sem=s1.at[h, i], recv_sem=r1.at[h, i], device_id=(a, p), device_id_type=MESH,
+            src_ref=sent.at[rows_of(p, tile, count), :], dst_ref=got.at[rows_of(s, tile, count), :],
+            send_sem=s1.at[0], recv_sem=r1.at[u], device_id=(a, p), device_id_type=MESH,
         )
 
-    def acq_copy(h, i):
+    def acq_copy(u, tile, count, i):
         p = lax.rem(a + i, DEV)
         return pltpu.make_async_remote_copy(
-            src_ref=scene.at[pl.ds(pl.multiple_of(128 * p + WIDE * h, WIDE), WIDE), :],
-            dst_ref=stack.at[pl.ds(pl.multiple_of(128 * a + WIDE * h, WIDE), WIDE), :],
-            send_sem=s2.at[h, i], recv_sem=r2.at[h, i], device_id=(p, s), device_id_type=MESH,
+            src_ref=scene.at[rows_of(p, tile, count), :], dst_ref=stack.at[rows_of(a, tile, count), :],
+            send_sem=s2.at[0], recv_sem=r2.at[u], device_id=(p, s), device_id_type=MESH,
         )
 
     def weight_copy(i):
         p = lax.rem(a + i, DEV)
         return pltpu.make_async_remote_copy(
             src_ref=wmine, dst_ref=wall.at[pl.ds(pl.multiple_of(8 * a, 8), 8), :],
-            send_sem=s3.at[i], recv_sem=r3.at[i], device_id=(p, s), device_id_type=MESH,
+            send_sem=s3.at[0], recv_sem=r3.at[0], device_id=(p, s), device_id_type=MESH,
         )
 
     def part_copy(i):
@@ -319,115 +320,134 @@
         return pltpu.make_async_remote_copy(
             src_ref=part_s.at[pl.ds(pl.multiple_of(8 * p, 8), 8), :],
             dst_ref=part_r.at[pl.ds(pl.multiple_of(8 * a, 8), 8), :],
-            send_sem=s4.at[i], recv_sem=r4.at[i], device_id=(p, s), device_id_type=MESH,
+            send_sem=s3.at[1], recv_sem=r3.at[1], device_id=(p, s), device_id_type=MESH,
         )
 
-    def first_send(i, _):
-        p = lax.rem(s + i, DEV)
-        at = pl.ds(pl.multiple_of(128 * p, 128), 128)
-        sent[at, :] = turned[at, :].T
-        strip_copy(0, i).start()
-        return 0
-
-    lax.fori_loop(1, DEV, first_send, 0)
-    for h in range(1, CHUNKS):
-        lax.fori_loop(1, DEV, lambda i, _, h=h: (strip_copy(h, i).start(), 0)[1], 0)
-    lax.fori_loop(1, DEV, lambda i, _: (weight_copy(i).start(), 0)[1], 0)
+    def wait_rows(ref, count, sem):
+        rows = ref.at[pl.ds(0, 15 * count), :]
+        pltpu.make_async_copy(rows, rows, sem).wait()
+
+    def others(body):
+        def step(i, _):
+            body(i)
+            return 0
+
+        lax.fori_loop(1, DEV, step, 0)
+
+    for n in range(16):
+        sent[pl.ds(128 * n, 128), :] = turned[pl.ds(128 * n, 128), :].T
+    pl.semaphore_wait(barrier, 2 * (DEV - 1))
+    for u, (tile, count) in enumerate(UNITS):
+        others(lambda i, u=u, tile=tile, count=count: strip_copy(u, tile, count, i).start())
+    others(lambda i: weight_copy(i).start())
     own = pl.ds(pl.multiple_of(128 * s, 128), 128)
-    got[own, :] = turned[own, :].T
+    got[own, :] = sent[own, :]
     wall[pl.ds(pl.multiple_of(8 * a, 8), 8), :] = wmine[...]
 
-    for copy in loads[7:]:
+    for copy in loads[5:]:
         copy.wait()
 
     def turn_filter(k, _):
         re, im = af[0, pl.ds(k, 64, stride=16), :], af[1, pl.ds(k, 64, stride=16), :]
-        c = dot_nt(pick[...], jnp.concatenate([re, re], axis=0))
-        t = dot_nt(pick[...], jnp.concatenate([-im, im], axis=0))
-        for h in range(CHUNKS):
-            at = pl.ds(pl.multiple_of(512 * h + WIDE * k, WIDE), WIDE)
-            fcos[at, :] = c[WIDE * h : WIDE * h + WIDE, :]
-            fsin[at, :] = t[WIDE * h : WIDE * h + WIDE, :]
+        both = jnp.concatenate([re, im], axis=0)
+        b0 = both.astype(jnp.bfloat16)
+        left = both - b0.astype(F32)
+        b1 = left.astype(jnp.bfloat16)
+        b2 = (left - b1.astype(F32)).astype(jnp.bfloat16)
+        v = dot_nt(pick[...], jnp.concatenate([b0, b1, b2], axis=1), None)
+        w = swapped(v)
+        first = lax.broadcasted_iota(jnp.int32, (128, 128), 1) < 64
+        c = jnp.where(first, v, w)
+        t = jnp.where(first, -w, v)
+        for q in range(TILES):
+            at = pl.ds(pl.multiple_of(128 * q + 8 * k, 8), 8)
+            fcos[at, :] = c[8 * q : 8 * q + 8, :]
+            fsin[at, :] = t[8 * q : 8 * q + 8, :]
         return 0
 
     lax.fori_loop(0, 16, turn_filter, 0)
 
-    lax.fori_loop(1, DEV, lambda i, _: (weight_copy(i).wait_recv(), 0)[1], 0)
+    wait_rows(wall, 8, r3.at[0])
     for l in range(2):
         columns = wall[pl.ds(l, 16, stride=8), :]
         for e in range(DEV):
             wide[pl.ds(16 * (16 * l + e), 16), :] = jnp.broadcast_to(columns[:, e : e + 1], (16, LANES))
 
-    def azimuth(h):
-        def forward(m, _):
-            field = [got[pl.ds(pl.multiple_of(128 * n + WIDE * h + 8 * m, 8), 8), :] for n in range(16)]
+    def azimuth(tile, count):
+        for m in range(count):
+            field = [got[rows_of(n, tile + m, 1), :] for n in range(16)]
             for k, v in enumerate(packed_dft16(field, -1.0, -half)):
                 v = v * tp[pl.ds(k, 1), :] + swapped(v) * tp[pl.ds(16 + k, 1), :]
-                mid[pl.ds(pl.multiple_of(WIDE * k + 8 * m, 8), 8), :] = v
-            return 0
-
-        lax.fori_loop(0, 4, forward, 0)
-        at = pl.ds(pl.multiple_of(512 * h, 512), 512)
-        z = dot_square(mid[...], w3[...])
+                mid[pl.ds(128 * m + 8 * k, 8), :] = v
+        at = pl.ds(pl.multiple_of(128 * tile, 128), 128 * count)
+        z = dot_square(mid[pl.ds(0, 128 * count), :], w3[...])
         z = z * fcos[at, :] + swapped(z) * fsin[at, :]
         z = dot_square(z, w4[...])
         z2 = swapped(z)
-        for k in range(16):
-            piece = slice(WIDE * k, WIDE * k + WIDE)
-            mid[pl.ds(WIDE * k, WIDE), :] = (
-                z[piece, :] * tp[pl.ds(32 + k, 1), :] + z2[piece, :] * tp[pl.ds(48 + k, 1), :]
-            )
-
-        def inverse(m, _):
-            field = [mid[pl.ds(pl.multiple_of(WIDE * k + 8 * m, 8), 8), :] for k in range(16)]
+        for m in range(count):
+            field = []
+            for k in range(16):
+                piece = slice(128 * m + 8 * k, 128 * m + 8 * k + 8)
+                field.append(z[piece, :] * tp[pl.ds(32 + k, 1), :] + z2[piece, :] * tp[pl.ds(48 + k, 1), :])
             for n, v in enumerate(packed_dft16(field, 1.0, half)):
-                scene[pl.ds(pl.multiple_of(128 * n + WIDE * h + 8 * m, 8), 8), :] = v
-            return 0
-
-        lax.fori_loop(0, 4, inverse, 0)
-
-    def products(h):
+                scene[rows_of(n, tile + m, 1), :] = v
+
+    def products(tile, count):
         held = {}
         for j in range(DEV):
-            held[j] = [stack[pl.ds(pl.multiple_of(128 * j + WIDE * h + 8 * m, 8), 8), :] for m in range(4)]
+            held[j] = [stack[rows_of(j, tile + m, 1), :] for m in range(count)]
             later = [swapped(v) for v in held[j]]
             for l in (1, 2):
                 if j >= l:
-                    same, cross = 0.0, 0.0
-                    for m in range(4):
-                        same = same + held[j - l][m] * held[j][m]
-                        cross = cross + held[j - l][m] * later[m]
+                    same, cross = None, None
+                    for m in range(count):
+                        v, w = held[j - l][m] * held[j][m], held[j - l][m] * later[m]
+                        same, cross = (v, w) if same is None else (same + v, cross + w)
                     p = PAIRS.index((l, j))
                     prod[pl.ds(8 * p, 8), pl.ds(0, 128)] = same
                     prod[pl.ds(8 * p, 8), pl.ds(128, 128)] = cross
-        pooled = dot(jnp.concatenate(halves(prod[...]), axis=1), pool[pl.ds(pl.multiple_of(512 * h, 512), 512), :])
-
-        @pl.when(h == 0)
+        block = pl.ds(pl.multiple_of(512 * (tile // 4), 512), 512)
+        pooled = dot(jnp.concatenate(halves(prod[...]), axis=1), pool[block, :])
+        look[...] += pooled
+
+    def focus(u, tile, count):
+        wait_rows(got, 8 * count, r1.at[u])
+        azimuth(tile, count)
+        others(lambda i: acq_copy(u, tile, count, i).start())
+        stack[rows_of(a, tile, count), :] = scene[rows_of(a, tile, count), :]
+
+    def combine(u, tile, count):
+        wait_rows(stack, 8 * count, r2.at[u])
+        products(tile, count)
+
+    look[...] = jnp.zeros_like(look)
+
+    def turn(u, _):
+        focus(u, 2 * u, 2)
+
+        @pl.when(u >= LAG)
         def _():
-            look[...] = pooled
-
-        @pl.when(h > 0)
-        def _():
-            look[...] += pooled
-
-    def turn(h, _):
-        @pl.when(h < CHUNKS)
-        def _():
-            lax.fori_loop(1, DEV, lambda i, _: (strip_copy(h, i).wait_recv(), 0)[1], 0)
-            azimuth(h)
-            lax.fori_loop(1, DEV, lambda i, _: (acq_copy(h, i).start(), 0)[1], 0)
-            stack[pl.ds(pl.multiple_of(128 * a + WIDE * h, WIDE), WIDE), :] = scene[
-                pl.ds(pl.multiple_of(128 * a + WIDE * h, WIDE), WIDE), :
-            ]
-
-        @pl.when(h > 0)
-        def _():
-            lax.fori_loop(1, DEV, lambda i, _: (acq_copy(h - 1, i).wait_recv(), 0)[1], 0)
-            products(h - 1)
+            combine(u - LAG, 2 * (u - LAG), 2)
 
         return 0
 
-    lax.fori_loop(0, CHUNKS + 1, turn, 0)
+    lax.fori_loop(0, PAIR_UNITS, turn, 0)
+
+    low_s[...] = jnp.zeros_like(low_s)
+    low_s[pl.ds(0, len(PAIRS)), :] = look[pl.ds(0, len(PAIRS), stride=8), :]
+    low_copy = pltpu.make_async_remote_copy(
+        src_ref=low_s, dst_ref=low_r, send_sem=s3.at[2], recv_sem=r3.at[2],
+        device_id=(a, lax.rem(s + DEV - 1, DEV)), device_id_type=MESH,
+    )
+
+    @pl.when(s > 0)
+    def _():
+        low_copy.start()
+
+    for u in range(PAIR_UNITS, len(UNITS)):
+        focus(u, *UNITS[u])
+    for u in range(PAIR_UNITS - LAG, len(UNITS)):
+        combine(u, *UNITS[u])
 
     side = [jnp.zeros((8, LANES), F32), jnp.zeros((8, LANES), F32)]
     for p in range(len(PAIRS)):
@@ -436,22 +456,25 @@
         side[p // 16] = jnp.where(lane % 16 == p % 16, v, side[p // 16])
     side_s[pl.ds(0, 8), :] = side[0]
     side_s[pl.ds(8, 8), :] = side[1]
-    low_s[pl.ds(0, len(PAIRS)), :] = look[pl.ds(0, len(PAIRS), stride=8), :]
     side_copy = pltpu.make_async_remote_copy(
-        src_ref=side_s, dst_ref=side_r, send_sem=s5.at[0], recv_sem=r5.at[0],
+        src_ref=side_s, dst_ref=side_r, send_sem=s3.at[3], recv_sem=r3.at[3],
         device_id=(lax.rem(a + DEV - 1, DEV), s), device_id_type=MESH,
     )
-    low_copy = pltpu.make_async_remote_copy(
-        src_ref=low_s.at[pl.ds(0, len(PAIRS)), :], dst_ref=low_r.at[pl.ds(0, len(PAIRS)), :], send_sem=s5.at[1], recv_sem=r5.at[1],
-        device_id=(a, lax.rem(s + DEV - 1, DEV)), device_id_type=MESH,
-    )
-    side_copy.start()
-    low_copy.start()
-    side_copy.wait_recv()
-    low_copy.wait_recv()
-
     inner = a < DEV - 1
     above = s < DEV - 1
+
+    @pl.when(a > 0)
+    def _():
+        side_copy.start()
+
+    @pl.when(inner)
+    def _():
+        side_copy.wait_recv()
+
+    @pl.when(above)
+    def _():
+        low_copy.wait_recv()
+
     border = [jnp.where(inner, side_r[pl.ds(8 * i, 8), :], 0.0) for i in range(2)]
     low_r[...] = jnp.where(above, pltpu.roll(low_r[...], 112, 1), 0.0)
     last_look = lane % 16 == 15
@@ -478,10 +501,10 @@
             total[e] = term if total[e] is None else total[e] + term
     for e in range(DEV):
         part_s[pl.ds(8 * e, 8), :] = total[e]
-    lax.fori_loop(1, DEV, lambda i, _: (part_copy(i).start(), 0)[1], 0)
+    others(lambda i: part_copy(i).start())
     mine = pl.ds(pl.multiple_of(8 * a, 8), 8)
     part_r[mine, :] = part_s[mine, :]
-    lax.fori_loop(1, DEV, lambda i, _: (part_copy(i).wait_recv(), 0)[1], 0)
+    wait_rows(part_r, 8, r3.at[1])
 
     for d in range(2):
         for h in range(CHUNKS):
@@ -494,13 +517,18 @@
                     tile = v if tile is None else jnp.where(lane // 16 == t, v, tile)
                 out[0, d, pl.ds(8 * h, 8), pl.ds(128 * u, 128)] = tile
 
-    for h in range(CHUNKS):
-        lax.fori_loop(1, DEV, lambda i, _, h=h: (strip_copy(h, i).wait_send(), 0)[1], 0)
-        lax.fori_loop(1, DEV, lambda i, _, h=h: (acq_copy(h, i).wait_send(), 0)[1], 0)
-    lax.fori_loop(1, DEV, lambda i, _: (weight_copy(i).wait_send(), 0)[1], 0)
-    lax.fori_loop(1, DEV, lambda i, _: (part_copy(i).wait_send(), 0)[1], 0)
-    side_copy.wait_send()
-    low_copy.wait_send()
+    wait_rows(sent, 128, s1.at[0])
+    wait_rows(scene, 128, s2.at[0])
+    wait_rows(wall, 8, s3.at[0])
+    wait_rows(part_s, 8, s3.at[1])
+
+    @pl.when(a > 0)
+    def _():
+        side_copy.wait_send()
+
+    @pl.when(s > 0)
+    def _():
+        low_copy.wait_send()
 
 
 def per_device(raw_echoes, range_filter, azimuth_filter, pair_mask, inversion):
@@ -518,12 +546,11 @@
         + [pltpu.VMEM(c.shape, c.dtype) for c in consts]
         + [
             vmem(1024, 256), vmem(32, 256), vmem(2048, 128), vmem(2048, 128), vmem(2048, 128),
-            vmem(512, 128), vmem(2048, 128), vmem(2048, 128), vmem(2048, 128), vmem(2048, 128),
+            vmem(256, 128), vmem(2048, 128), vmem(2048, 128), vmem(2048, 128), vmem(2048, 128),
             vmem(ROWS, 256), vmem(ROWS, 128),
             vmem(8, 128), vmem(128, 128), vmem(512, 128), vmem(16, 128), vmem(16, 128), vmem(32, 128), vmem(32, 128),
             vmem(ROWS, 128), vmem(128, 128), vmem(128, 128),
-            dma((13,)), dma((8,)), dma((CHUNKS, DEV)), dma((CHUNKS, DEV)), dma((CHUNKS, DEV)), dma((CHUNKS, DEV)),
-            dma((DEV,)), dma((DEV,)), dma((DEV,)), dma((DEV,)), dma((2,)), dma((2,)),
+            dma((11,)), dma((8,)), dma((1,)), dma((len(UNITS),)), dma((1,)), dma((len(UNITS),)), dma((4,)), dma((4,)),
         ],
         compiler_params=pltpu.CompilerParams(collective_id=0, has_side_effects=True, vmem_limit_bytes=60 * 1024 * 1024),
     )(raw_echoes, range_filter, azimuth_filter, inversion[:, 0, :].T, pair_mask, *[jnp.asarray(c) for c in consts])

time: 59.8 us -> 53.6 us (0.90)
  Pallas kernels: 58.2 us -> 52 us
    pallas_call x1, Pallas kernels: 58.2 us -> 52 us  [per_device(): pl.pallas_call(kernel, out_shape=jax.ShapeDtypeStruct((1, 2, WIDE, 256),...]
where the time goes in v1:
time: 53.6 us; the launch traced here: 53.5 us
  Pallas kernels  52 us (97%)
  local copies, waits for them, and re-layouts  1.47 us (3%)
    pallas_call x1, Pallas kernels, per_device(): pl.pallas_call(kernel, out_shape=jax.ShapeDtypeStruct((1, 2, WIDE, 256),...  52 us
    unnamed x1, local copies, waits for them, and re-layouts  1.47 us

profile of v1, /device:TPU:1, one launch (start us, length us, event | category | flops | bytes accessed | tf_op | source)
XLA Modules:
  0.0 53.5 jit_solution(852005969584537240)
XLA Ops:
  0.0 52.0 %shard_map.127 = f32[1,2,32,256]{3,2,1,0:T(8,128)} custom-call(f32[1,2,64,2048]{3,2,1,0:T(8,128)} %raw.1, f32[2,2048]{1,0:T(2,128)} %rfil.1, f32[2,1024,128]{2,1,0:T(8,128)} %afil.1, f32[2,16]{1,0:T(2,128)} %bitcast.3, s32[1,2]{1,0:T(1,128)} %mask.1, bf16[768,256]{1,0:T(8,128)(2,1)} %constant.16.clone.w1_h, bf16[768,256]{1,0:T(8,128)(2,1)} %constant.17.clone.w2_h, ...), custom_call_target="tpu_custom_call" | custom-call | tf_op jit(solution)/shard_map/pallas_call | solution.py:540
  52.0 1.5 %copy.15 = f32[1,2,32,256]{3,2,1,0:T(8,128)} copy(f32[1,2,32,256]{3,2,1,0:T(8,128)} %shard_map.127) | data formatting | bytes 131072

commit v2 on v1

--- a/solution.py
+++ b/solution.py
@@ -14,13 +14,13 @@
 F32 = jnp.float32
 LANES = 128
 DEV = 16
+ORDER = (8, 7, 9, 6, 10, 5, 11, 4, 12, 3, 13, 2, 14, 1, 15)
 Q = 64
 CHUNKS = 4
 WIDE = 32
 TILES = 16
-PAIR_UNITS = 7
-LAG = 3
-UNITS = [(2 * u, 2) for u in range(PAIR_UNITS)] + [(t, 1) for t in range(2 * PAIR_UNITS, TILES)]
+LONG = 3
+UNITS = [(4 * u, 4) for u in range(LONG)] + [(12, 2), (14, 1), (15, 1)]
 PAIRS = [(1, j) for j in range(1, DEV)] + [(2, j) for j in range(2, DEV)]
 ROWS = 8 * len(PAIRS)
 
@@ -61,7 +61,7 @@
     turn_pulse = np.concatenate(
         [np.hstack([c3, c3]), np.hstack([-s3, s3]), np.hstack([c4, c4]), np.hstack([-s4, s4])]
     )
-    pool = np.zeros((CHUNKS, 256, LANES))
+    pool = np.zeros((CHUNKS + 1, 256, LANES))
     for h in range(CHUNKS):
         for q in range(Q):
             real, imag = 16 * h + q // 4, 64 + 16 * h + q // 4
@@ -69,6 +69,10 @@
             pool[h, 64 + q, real] = 0.25
             pool[h, 128 + q, imag] = -0.25
             pool[h, 192 + q, imag] = 0.25
+    for lane in range(LANES):
+        at = 16 * (lane // 32) + 15
+        pool[CHUNKS, lane, 64 + at] = 0.25
+        pool[CHUNKS, 128 + lane, at] = -0.25 if lane % 8 < 4 else 0.25
     pick = np.zeros((LANES, LANES))
     pick[np.arange(LANES), order] = 1.0
     def split(w):
@@ -180,12 +184,12 @@
 
 
 def kernel(
-    raw, rfil, afil, inv, mask,
+    raw, rfil, afil, inv, flags,
     w1_h, w2_h, tr_h, w3_h, w4_h, tp_h, pool_h, pick_h,
     out,
-    x, rf, af, iv, w1, w2, tr, w3, w4, tp, pool, pick,
-    spec, gain, turned, sent, got, mid, fcos, fsin, scene, stack, prod, look,
-    wmine, wall, wide, side_s, side_r, low_s, low_r, slope, part_s, part_r,
+    x, rf, af, iv, mask, w1, w2, tr, w3, w4, tp, pool, pick,
+    spec, gain, turned, sent, got, fcos, fsin, scene, stack, prod, look,
+    wmine, wall, wide, edge_s, edge_r, border, low_s, low_r, slope, part_s, part_r,
     ld, ldx, s1, r1, s2, r2, s3, r3,
 ):
     a, s = lax.axis_index("acq"), lax.axis_index("strip")
@@ -206,15 +210,15 @@
     loads = [
         pltpu.make_async_copy(src, dst, ld.at[i])
         for i, (src, dst) in enumerate([
-            (rfil, rf), (inv, iv), (tr_h, tr), (w1_h, w1), (w2_h, w2),
-            (pick_h, pick), (afil, af), (w3_h, w3), (w4_h, w4), (tp_h, tp), (pool_h, pool),
+            (rfil, rf), (tr_h, tr), (w1_h, w1), (w2_h, w2),
+            (pick_h, pick), (afil, af), (inv, iv), (flags, mask), (w3_h, w3), (w4_h, w4), (tp_h, tp), (pool_h, pool),
         ])
     ]
-    for copy in loads[:3]:
+    for copy in loads[:2]:
         copy.start()
     for g in range(8):
         load_x(g).start()
-    for copy in loads[3:]:
+    for copy in loads[2:]:
         copy.start()
 
     lane = lax.broadcasted_iota(jnp.int32, (8, LANES), 1)
@@ -222,11 +226,6 @@
     half = jnp.where(lane < 64, -1.0, 1.0).astype(F32)
 
     loads[0].wait()
-    loads[1].wait()
-    usable = [jnp.where(a >= l + 1, mask[0, l].astype(F32), 0.0) for l in range(2)]
-    wmine[...] = jnp.zeros((8, LANES), F32)
-    for l in range(2):
-        wmine[pl.ds(l, 1), pl.ds(0, DEV)] = iv[pl.ds(l, 1), :] * usable[l]
 
     for c in range(2):
         for k in range(16):
@@ -241,7 +240,7 @@
         part = dot(across[16 * m : 16 * m + 16, :], place, EXACT)
         ordered = part if ordered is None else ordered + part
     gain[pl.ds(0, 16), :] = ordered
-    loads[2].wait()
+    loads[1].wait()
 
     def forward_range(g, _):
         load_x(g).wait()
@@ -256,7 +255,7 @@
 
     lax.fori_loop(0, 8, forward_range, 0, unroll=2)
 
-    for copy in loads[3:5]:
+    for copy in loads[2:4]:
         copy.wait()
 
     def filter_range(k, _):
@@ -323,28 +322,31 @@
             send_sem=s3.at[1], recv_sem=r3.at[1], device_id=(p, s), device_id_type=MESH,
         )
 
+    def edge_copy(i):
+        p = lax.rem(a + i, DEV)
+        return pltpu.make_async_remote_copy(
+            src_ref=edge_s.at[pl.ds(pl.multiple_of(8 * p, 8), 8), :],
+            dst_ref=edge_r.at[pl.ds(pl.multiple_of(8 * a, 8), 8), :],
+            send_sem=s3.at[3], recv_sem=r3.at[3], device_id=(p, s), device_id_type=MESH,
+        )
+
     def wait_rows(ref, count, sem):
         rows = ref.at[pl.ds(0, 15 * count), :]
         pltpu.make_async_copy(rows, rows, sem).wait()
 
     def others(body):
-        def step(i, _):
+        for i in ORDER:
             body(i)
-            return 0
-
-        lax.fori_loop(1, DEV, step, 0)
 
     for n in range(16):
         sent[pl.ds(128 * n, 128), :] = turned[pl.ds(128 * n, 128), :].T
     pl.semaphore_wait(barrier, 2 * (DEV - 1))
     for u, (tile, count) in enumerate(UNITS):
         others(lambda i, u=u, tile=tile, count=count: strip_copy(u, tile, count, i).start())
-    others(lambda i: weight_copy(i).start())
     own = pl.ds(pl.multiple_of(128 * s, 128), 128)
     got[own, :] = sent[own, :]
-    wall[pl.ds(pl.multiple_of(8 * a, 8), 8), :] = wmine[...]
-
-    for copy in loads[5:]:
+
+    for copy in loads[4:]:
         copy.wait()
 
     def turn_filter(k, _):
@@ -367,20 +369,22 @@
 
     lax.fori_loop(0, 16, turn_filter, 0)
 
-    wait_rows(wall, 8, r3.at[0])
+    usable = [jnp.where(a >= l + 1, mask[0, l].astype(F32), 0.0) for l in range(2)]
+    wmine[...] = jnp.zeros((8, LANES), F32)
     for l in range(2):
-        columns = wall[pl.ds(l, 16, stride=8), :]
-        for e in range(DEV):
-            wide[pl.ds(16 * (16 * l + e), 16), :] = jnp.broadcast_to(columns[:, e : e + 1], (16, LANES))
+        wmine[pl.ds(l, 1), pl.ds(0, DEV)] = iv[pl.ds(l, 1), :] * usable[l]
+
+    others(lambda i: weight_copy(i).start())
+    wall[pl.ds(pl.multiple_of(8 * a, 8), 8), :] = wmine[...]
 
     def azimuth(tile, count):
+        parts = []
         for m in range(count):
             field = [got[rows_of(n, tile + m, 1), :] for n in range(16)]
             for k, v in enumerate(packed_dft16(field, -1.0, -half)):
-                v = v * tp[pl.ds(k, 1), :] + swapped(v) * tp[pl.ds(16 + k, 1), :]
-                mid[pl.ds(128 * m + 8 * k, 8), :] = v
+                parts.append(v * tp[pl.ds(k, 1), :] + swapped(v) * tp[pl.ds(16 + k, 1), :])
         at = pl.ds(pl.multiple_of(128 * tile, 128), 128 * count)
-        z = dot_square(mid[pl.ds(0, 128 * count), :], w3[...])
+        z = dot_square(jnp.concatenate(parts, axis=0), w3[...])
         z = z * fcos[at, :] + swapped(z) * fsin[at, :]
         z = dot_square(z, w4[...])
         z2 = swapped(z)
@@ -391,6 +395,15 @@
                 field.append(z[piece, :] * tp[pl.ds(32 + k, 1), :] + z2[piece, :] * tp[pl.ds(48 + k, 1), :])
             for n, v in enumerate(packed_dft16(field, 1.0, half)):
                 scene[rows_of(n, tile + m, 1), :] = v
+
+    def edges(tile, count):
+        for m in range(count):
+            t = tile + m
+            for n in range(1, 16):
+                v = scene[rows_of(n, t, 1), :]
+                v = jnp.where(lane % 8 < 4, pltpu.roll(v, 8 * t, 1), pltpu.roll(v, lax.rem(8 * t + 68, 128), 1))
+                at = pl.ds(8 * (n - 1), 8)
+                edge_s[at, :] = jnp.where(lane // 8 == t, v, edge_s[at, :])
 
     def products(tile, count):
         held = {}
@@ -414,6 +427,7 @@
         wait_rows(got, 8 * count, r1.at[u])
         azimuth(tile, count)
         others(lambda i: acq_copy(u, tile, count, i).start())
+        edges(tile, count)
         stack[rows_of(a, tile, count), :] = scene[rows_of(a, tile, count), :]
 
     def combine(u, tile, count):
@@ -421,17 +435,18 @@
         products(tile, count)
 
     look[...] = jnp.zeros_like(look)
+    edge_s[...] = jnp.zeros_like(edge_s)
 
     def turn(u, _):
-        focus(u, 2 * u, 2)
-
-        @pl.when(u >= LAG)
+        focus(u, 4 * u, 4)
+
+        @pl.when(u == 1)
         def _():
-            combine(u - LAG, 2 * (u - LAG), 2)
+            combine(0, 0, 4)
 
         return 0
 
-    lax.fori_loop(0, PAIR_UNITS, turn, 0)
+    lax.fori_loop(0, LONG, turn, 0)
 
     low_s[...] = jnp.zeros_like(low_s)
     low_s[pl.ds(0, len(PAIRS)), :] = look[pl.ds(0, len(PAIRS), stride=8), :]
@@ -444,46 +459,41 @@
     def _():
         low_copy.start()
 
-    for u in range(PAIR_UNITS, len(UNITS)):
+    for u in range(LONG, len(UNITS)):
         focus(u, *UNITS[u])
-    for u in range(PAIR_UNITS - LAG, len(UNITS)):
+    others(lambda i: edge_copy(i).start())
+    mine = pl.ds(pl.multiple_of(8 * a, 8), 8)
+    edge_r[mine, :] = edge_s[mine, :]
+    wait_rows(wall, 8, r3.at[0])
+    for l in range(2):
+        columns = wall[pl.ds(l, 16, stride=8), :]
+        for e in range(DEV):
+            wide[pl.ds(16 * (16 * l + e), 16), :] = jnp.broadcast_to(columns[:, e : e + 1], (16, LANES))
+
+    for u in range(1, len(UNITS)):
         combine(u, *UNITS[u])
 
-    side = [jnp.zeros((8, LANES), F32), jnp.zeros((8, LANES), F32)]
-    for p in range(len(PAIRS)):
-        v = look[pl.ds(8 * p, 8), :]
-        v = pltpu.roll(v, p % 16, 1) if p % 16 else v
-        side[p // 16] = jnp.where(lane % 16 == p % 16, v, side[p // 16])
-    side_s[pl.ds(0, 8), :] = side[0]
-    side_s[pl.ds(8, 8), :] = side[1]
-    side_copy = pltpu.make_async_remote_copy(
-        src_ref=side_s, dst_ref=side_r, send_sem=s3.at[3], recv_sem=r3.at[3],
-        device_id=(lax.rem(a + DEV - 1, DEV), s), device_id_type=MESH,
-    )
-    inner = a < DEV - 1
+    wait_rows(edge_r, 8, r3.at[3])
+    edge = [edge_r[pl.ds(8 * j, 8), :] for j in range(DEV)]
+    turned_edge = [jnp.where(lane % 8 < 4, pltpu.roll(v, 124, 1), pltpu.roll(v, 4, 1)) for v in edge]
+    for p, (l, j) in enumerate(PAIRS):
+        prod[pl.ds(8 * p, 8), pl.ds(0, 128)] = edge[j - l] * edge[j]
+        prod[pl.ds(8 * p, 8), pl.ds(128, 128)] = edge[j - l] * turned_edge[j]
+    border[...] = dot(jnp.concatenate(halves(prod[...]), axis=1), pool[pl.ds(512 * CHUNKS, 512), :])
+
     above = s < DEV - 1
-
-    @pl.when(a > 0)
-    def _():
-        side_copy.start()
-
-    @pl.when(inner)
-    def _():
-        side_copy.wait_recv()
 
     @pl.when(above)
     def _():
         low_copy.wait_recv()
 
-    border = [jnp.where(inner, side_r[pl.ds(8 * i, 8), :], 0.0) for i in range(2)]
     low_r[...] = jnp.where(above, pltpu.roll(low_r[...], 112, 1), 0.0)
     last_look = lane % 16 == 15
     corner = (row8 == 7) & (lane % 64 >= 48)
     for p in range(len(PAIRS)):
         v = look[pl.ds(8 * p, 8), :]
         after = pltpu.roll(v, 63, 1)
-        edge = pltpu.roll(border[p // 16], (64 + 15 - p % 16) % 128, 1)
-        after = jnp.where(last_look, edge, after)
+        after = jnp.where(last_look, border[pl.ds(8 * p, 8), :], after)
         up = jnp.where(row8 == 0, pltpu.roll(v, 48, 1), pltpu.roll(v, 64, 1))
         up = pltpu.roll(up, 7, 0)
         up = jnp.where(corner, jnp.broadcast_to(low_r[pl.ds(p, 1), :], (8, LANES)), up)
@@ -502,7 +512,6 @@
     for e in range(DEV):
         part_s[pl.ds(8 * e, 8), :] = total[e]
     others(lambda i: part_copy(i).start())
-    mine = pl.ds(pl.multiple_of(8 * a, 8), 8)
     part_r[mine, :] = part_s[mine, :]
     wait_rows(part_r, 8, r3.at[1])
 
@@ -521,10 +530,7 @@
     wait_rows(scene, 128, s2.at[0])
     wait_rows(wall, 8, s3.at[0])
     wait_rows(part_s, 8, s3.at[1])
-
-    @pl.when(a > 0)
-    def _():
-        side_copy.wait_send()
+    wait_rows(edge_s, 8, s3.at[3])
 
     @pl.when(s > 0)
     def _():
@@ -534,23 +540,22 @@
 def per_device(raw_echoes, range_filter, azimuth_filter, pair_mask, inversion):
     consts = tables()
     hbm = pl.BlockSpec(memory_space=pl.ANY)
-    smem = pl.BlockSpec(memory_space=pltpu.SMEM)
     vmem = lambda *shape: pltpu.VMEM(shape, F32)
     dma = pltpu.SemaphoreType.DMA
     return pl.pallas_call(
         kernel,
-        out_shape=jax.ShapeDtypeStruct((1, 2, WIDE, 256), F32),
-        in_specs=[hbm, hbm, hbm, hbm, smem] + [hbm] * len(consts),
+        out_shape=pltpu.VMEM((1, 2, WIDE, 256), F32),
+        in_specs=[hbm] * 5 + [hbm] * len(consts),
         out_specs=pl.BlockSpec(memory_space=pltpu.VMEM),
-        scratch_shapes=[vmem(2, 64, 2048), vmem(2, 2048), vmem(2, 1024, 128), vmem(2, DEV)]
+        scratch_shapes=[vmem(2, 64, 2048), vmem(2, 2048), vmem(2, 1024, 128), vmem(2, DEV), pltpu.SMEM((1, 2), jnp.int32)]
         + [pltpu.VMEM(c.shape, c.dtype) for c in consts]
         + [
             vmem(1024, 256), vmem(32, 256), vmem(2048, 128), vmem(2048, 128), vmem(2048, 128),
-            vmem(256, 128), vmem(2048, 128), vmem(2048, 128), vmem(2048, 128), vmem(2048, 128),
+            vmem(2048, 128), vmem(2048, 128), vmem(2048, 128), vmem(2048, 128),
             vmem(ROWS, 256), vmem(ROWS, 128),
-            vmem(8, 128), vmem(128, 128), vmem(512, 128), vmem(16, 128), vmem(16, 128), vmem(32, 128), vmem(32, 128),
+            vmem(8, 128), vmem(128, 128), vmem(512, 128), vmem(128, 128), vmem(128, 128), vmem(ROWS, 128), vmem(32, 128), vmem(32, 128),
             vmem(ROWS, 128), vmem(128, 128), vmem(128, 128),
-            dma((11,)), dma((8,)), dma((1,)), dma((len(UNITS),)), dma((1,)), dma((len(UNITS),)), dma((4,)), dma((4,)),
+            dma((12,)), dma((8,)), dma((1,)), dma((len(UNITS),)), dma((1,)), dma((len(UNITS),)), dma((4,)), dma((4,)),
         ],
         compiler_params=pltpu.CompilerParams(collective_id=0, has_side_effects=True, vmem_limit_bytes=60 * 1024 * 1024),
     )(raw_echoes, range_filter, azimuth_filter, inversion[:, 0, :].T, pair_mask, *[jnp.asarray(c) for c in consts])

time: 53.6 us -> 49.3 us (0.920)
  Pallas kernels: 52 us -> 48.5 us
  local copies, waits for them, and re-layouts: 1.47 us -> 0.63 us
    pallas_call x1, Pallas kernels: 52 us -> 48.5 us  [per_device(): pl.pallas_call(kernel, out_shape=pltpu.VMEM((1, 2, WIDE, 256), F32), in_s...]
    unnamed x1, local copies, waits for them, and re-layouts: 1.47 us -> 0.63 us
where the time goes in v2:
time: 49.3 us; the launch traced here: 49.1 us
  Pallas kernels  48.5 us (98%)
  local copies, waits for them, and re-layouts  0.63 us (1%)
    pallas_call x1, Pallas kernels, per_device(): pl.pallas_call(kernel, out_shape=pltpu.VMEM((1, 2, WIDE, 256), F32), in_s...  48.5 us

profile of v2, /device:TPU:1, one launch (start us, length us, event | category | flops | bytes accessed | tf_op | source)
XLA Modules:
  0.0 49.1 jit_solution(10182542950459018554)
XLA Ops:
  0.0 48.5 %shard_map.127 = f32[1,2,32,256]{3,2,1,0:T(8,128)S(1)} custom-call(f32[1,2,64,2048]{3,2,1,0:T(8,128)} %raw.1, f32[2,2048]{1,0:T(2,128)} %rfil.1, f32[2,1024,128]{2,1,0:T(8,128)} %afil.1, f32[2,16]{1,0:T(2,128)} %bitcast.3, s32[1,2]{1,0:T(1,128)} %flags.1, bf16[768,256]{1,0:T(8,128)(2,1)} %constant.16.clone.w1_h, bf16[768,256]{1,0:T(8,128)(2,1)} %constant.17.clone.w2_h, ...), custom_call_target="tpu_custom_call" | custom-call | tf_op jit(solution)/shard_map/pallas_call | solution.py:545
  48.5 0.6 %copy.15 = f32[1,2,32,256]{3,2,1,0:T(8,128)} copy(f32[1,2,32,256]{3,2,1,0:T(8,128)S(1)} %shard_map.127) | data formatting | bytes 131072

commit v3 on v2

--- a/solution.py
+++ b/solution.py
@@ -15,12 +15,13 @@
 LANES = 128
 DEV = 16
 ORDER = (8, 7, 9, 6, 10, 5, 11, 4, 12, 3, 13, 2, 14, 1, 15)
+ZS = 8
 Q = 64
 CHUNKS = 4
 WIDE = 32
 TILES = 16
 LONG = 3
-UNITS = [(4 * u, 4) for u in range(LONG)] + [(12, 2), (14, 1), (15, 1)]
+UNITS = [(4 * u, 4) for u in range(LONG)] + [(12, 3), (15, 1)]
 PAIRS = [(1, j) for j in range(1, DEV)] + [(2, j) for j in range(2, DEV)]
 ROWS = 8 * len(PAIRS)
 
@@ -188,20 +189,33 @@
     w1_h, w2_h, tr_h, w3_h, w4_h, tp_h, pool_h, pick_h,
     out,
     x, rf, af, iv, mask, w1, w2, tr, w3, w4, tp, pool, pick,
-    spec, gain, turned, sent, got, fcos, fsin, scene, stack, prod, look,
+    spec, gain, turned, sent, flip_s, flip_r, got, fcos, fsin, scene, stack, prod, cross, look,
     wmine, wall, wide, edge_s, edge_r, border, low_s, low_r, slope, part_s, part_r,
-    ld, ldx, s1, r1, s2, r2, s3, r3,
+    ld, ldx, s1, r1, s2, r2, s3, r3, s4, r4,
 ):
     a, s = lax.axis_index("acq"), lax.axis_index("strip")
 
+    z, xh = lax.rem(s, ZS), s // ZS
+    partner = (1 - xh) * ZS + z
+
     barrier = pltpu.get_barrier_semaphore()
 
-    def greet(i, _):
-        pl.semaphore_signal(barrier, inc=1, device_id=(a, lax.rem(s + i, DEV)), device_id_type=MESH)
-        pl.semaphore_signal(barrier, inc=1, device_id=(lax.rem(a + i, DEV), s), device_id_type=MESH)
-        return 0
-
-    lax.fori_loop(1, DEV, greet, 0, unroll=True)
+    def greet(device):
+        pl.semaphore_signal(barrier, inc=1, device_id=device, device_id_type=MESH)
+
+    for i in (4, 3, 5, 2, 6, 1, 7):
+        greet((a, xh * ZS + lax.rem(z + i, ZS)))
+    for i in ORDER:
+        greet((lax.rem(a + i, DEV), s))
+    greet((a, partner))
+
+    @pl.when(z == ZS - 1)
+    def _():
+        greet((a, (1 - xh) * ZS))
+
+    @pl.when(z == 0)
+    def _():
+        greet((a, (1 - xh) * ZS + ZS - 1))
 
     def load_x(g):
         rows = pl.ds(pl.multiple_of(8 * g, 8), 8)
@@ -293,11 +307,28 @@
     def rows_of(block, tile, count):
         return pl.ds(pl.multiple_of(128 * block + 8 * tile, 8), 8 * count)
 
-    def strip_copy(u, tile, count, i):
-        p = lax.rem(s + i, DEV)
+    def direct_copy(u, tile, count, i):
+        p = lax.rem(z + i, ZS)
         return pltpu.make_async_remote_copy(
             src_ref=sent.at[rows_of(p, tile, count), :], dst_ref=got.at[rows_of(s, tile, count), :],
-            send_sem=s1.at[0], recv_sem=r1.at[u], device_id=(a, p), device_id_type=MESH,
+            send_sem=s1.at[0], recv_sem=r1.at[u], device_id=(a, xh * ZS + p), device_id_type=MESH,
+        )
+
+    def flip_copy(u, tile, count):
+        rows = pl.ds(64 * tile, 64 * count)
+        return pltpu.make_async_remote_copy(
+            src_ref=flip_s.at[rows, :], dst_ref=flip_r.at[rows, :],
+            send_sem=s4.at[0], recv_sem=r4.at[u], device_id=(a, partner), device_id_type=MESH,
+        )
+
+    def flip_rows(tile, count, p):
+        return pl.ds(pl.multiple_of(64 * tile + 8 * count * p, 8), 8 * count)
+
+    def relay_copy(u, tile, count, i):
+        p = lax.rem(z + i, ZS)
+        return pltpu.make_async_remote_copy(
+            src_ref=flip_r.at[flip_rows(tile, count, p), :], dst_ref=got.at[rows_of(partner, tile, count), :],
+            send_sem=s1.at[0], recv_sem=r1.at[u], device_id=(a, xh * ZS + p), device_id_type=MESH,
         )
 
     def acq_copy(u, tile, count, i):
@@ -330,21 +361,39 @@
             send_sem=s3.at[3], recv_sem=r3.at[3], device_id=(p, s), device_id_type=MESH,
         )
 
-    def wait_rows(ref, count, sem):
-        rows = ref.at[pl.ds(0, 15 * count), :]
+    def wait_rows(ref, count, sem, times=DEV - 1):
+        rows = ref.at[pl.ds(0, times * count), :]
         pltpu.make_async_copy(rows, rows, sem).wait()
 
     def others(body):
         for i in ORDER:
             body(i)
 
-    for n in range(16):
-        sent[pl.ds(128 * n, 128), :] = turned[pl.ds(128 * n, 128), :].T
-    pl.semaphore_wait(barrier, 2 * (DEV - 1))
-    for u, (tile, count) in enumerate(UNITS):
-        others(lambda i, u=u, tile=tile, count=count: strip_copy(u, tile, count, i).start())
-    own = pl.ds(pl.multiple_of(128 * s, 128), 128)
-    got[own, :] = sent[own, :]
+    for n in range(ZS):
+        v = turned[pl.ds(pl.multiple_of(128 * (ZS * (1 - xh) + n), 128), 128), :].T
+        for tile, count in UNITS:
+            flip_s[pl.ds(64 * tile + 8 * count * n, 8 * count), :] = v[8 * tile : 8 * tile + 8 * count, :]
+    for n in range(ZS):
+        sent[pl.ds(128 * n, 128), :] = turned[pl.ds(pl.multiple_of(128 * (ZS * xh + n), 128), 128), :].T
+    pl.semaphore_wait(barrier, ZS + DEV - 1 + jnp.where((z == 0) | (z == ZS - 1), 1, 0))
+
+    def direct(u):
+        for i in (4, 3, 5, 2, 6, 1, 7):
+            direct_copy(u, *UNITS[u], i).start()
+
+    def relay(u):
+        tile, count = UNITS[u]
+        flip_copy(u, tile, count).wait_recv()
+        for i in (4, 3, 5, 2, 6, 1, 7):
+            relay_copy(u, tile, count, i).start()
+        got[rows_of(partner, tile, count), :] = flip_r[flip_rows(tile, count, z), :]
+
+    flip_copy(0, *UNITS[0]).start()
+    direct(0)
+    for u in range(1, len(UNITS)):
+        flip_copy(u, *UNITS[u]).start()
+    direct(1)
+    got[pl.ds(pl.multiple_of(128 * s, 128), 128), :] = sent[pl.ds(pl.multiple_of(128 * z, 128), 128), :]
 
     for copy in loads[4:]:
         copy.wait()
@@ -368,6 +417,13 @@
         return 0
 
     lax.fori_loop(0, 16, turn_filter, 0)
+
+    relay(0)
+    direct(2)
+    relay(1)
+    relay(2)
+    for u in range(LONG, len(UNITS)):
+        direct(u)
 
     usable = [jnp.where(a >= l + 1, mask[0, l].astype(F32), 0.0) for l in range(2)]
     wmine[...] = jnp.zeros((8, LANES), F32)
@@ -412,19 +468,19 @@
             later = [swapped(v) for v in held[j]]
             for l in (1, 2):
                 if j >= l:
-                    same, cross = None, None
+                    same, other = None, None
                     for m in range(count):
                         v, w = held[j - l][m] * held[j][m], held[j - l][m] * later[m]
-                        same, cross = (v, w) if same is None else (same + v, cross + w)
+                        same, other = (v, w) if same is None else (same + v, other + w)
                     p = PAIRS.index((l, j))
                     prod[pl.ds(8 * p, 8), pl.ds(0, 128)] = same
-                    prod[pl.ds(8 * p, 8), pl.ds(128, 128)] = cross
+                    prod[pl.ds(8 * p, 8), pl.ds(128, 128)] = other
         block = pl.ds(pl.multiple_of(512 * (tile // 4), 512), 512)
         pooled = dot(jnp.concatenate(halves(prod[...]), axis=1), pool[block, :])
         look[...] += pooled
 
     def focus(u, tile, count):
-        wait_rows(got, 8 * count, r1.at[u])
+        wait_rows(got, 8 * count, r1.at[u], 2 * ZS - 2)
         azimuth(tile, count)
         others(lambda i: acq_copy(u, tile, count, i).start())
         edges(tile, count)
@@ -439,6 +495,11 @@
 
     def turn(u, _):
         focus(u, 4 * u, 4)
+
+        @pl.when(u == 0)
+        def _():
+            for later in range(LONG, len(UNITS)):
+                relay(later)
 
         @pl.when(u == 1)
         def _():
@@ -470,16 +531,18 @@
         for e in range(DEV):
             wide[pl.ds(16 * (16 * l + e), 16), :] = jnp.broadcast_to(columns[:, e : e + 1], (16, LANES))
 
-    for u in range(1, len(UNITS)):
+    for u in range(1, len(UNITS) - 1):
         combine(u, *UNITS[u])
-
+    wait_rows(stack, 8 * UNITS[-1][1], r2.at[len(UNITS) - 1])
     wait_rows(edge_r, 8, r3.at[3])
+    products(*UNITS[-1])
+
     edge = [edge_r[pl.ds(8 * j, 8), :] for j in range(DEV)]
     turned_edge = [jnp.where(lane % 8 < 4, pltpu.roll(v, 124, 1), pltpu.roll(v, 4, 1)) for v in edge]
     for p, (l, j) in enumerate(PAIRS):
-        prod[pl.ds(8 * p, 8), pl.ds(0, 128)] = edge[j - l] * edge[j]
-        prod[pl.ds(8 * p, 8), pl.ds(128, 128)] = edge[j - l] * turned_edge[j]
-    border[...] = dot(jnp.concatenate(halves(prod[...]), axis=1), pool[pl.ds(512 * CHUNKS, 512), :])
+        cross[pl.ds(8 * p, 8), pl.ds(0, 128)] = edge[j - l] * edge[j]
+        cross[pl.ds(8 * p, 8), pl.ds(128, 128)] = edge[j - l] * turned_edge[j]
+    border[...] = dot(jnp.concatenate(halves(cross[...]), axis=1), pool[pl.ds(512 * CHUNKS, 512), :])
 
     above = s < DEV - 1
 
@@ -526,7 +589,8 @@
                     tile = v if tile is None else jnp.where(lane // 16 == t, v, tile)
                 out[0, d, pl.ds(8 * h, 8), pl.ds(128 * u, 128)] = tile
 
-    wait_rows(sent, 128, s1.at[0])
+    wait_rows(got, 128, s1.at[0], 2 * ZS - 2)
+    wait_rows(flip_s, 128, s4.at[0], ZS)
     wait_rows(scene, 128, s2.at[0])
     wait_rows(wall, 8, s3.at[0])
     wait_rows(part_s, 8, s3.at[1])
@@ -550,12 +614,12 @@
         scratch_shapes=[vmem(2, 64, 2048), vmem(2, 2048), vmem(2, 1024, 128), vmem(2, DEV), pltpu.SMEM((1, 2), jnp.int32)]
         + [pltpu.VMEM(c.shape, c.dtype) for c in consts]
         + [
-            vmem(1024, 256), vmem(32, 256), vmem(2048, 128), vmem(2048, 128), vmem(2048, 128),
+            vmem(1024, 256), vmem(32, 256), vmem(2048, 128), vmem(1024, 128), vmem(1024, 128), vmem(1024, 128), vmem(2048, 128),
             vmem(2048, 128), vmem(2048, 128), vmem(2048, 128), vmem(2048, 128),
-            vmem(ROWS, 256), vmem(ROWS, 128),
+            vmem(ROWS, 256), vmem(ROWS, 256), vmem(ROWS, 128),
             vmem(8, 128), vmem(128, 128), vmem(512, 128), vmem(128, 128), vmem(128, 128), vmem(ROWS, 128), vmem(32, 128), vmem(32, 128),
             vmem(ROWS, 128), vmem(128, 128), vmem(128, 128),
-            dma((12,)), dma((8,)), dma((1,)), dma((len(UNITS),)), dma((1,)), dma((len(UNITS),)), dma((4,)), dma((4,)),
+            dma((12,)), dma((8,)), dma((1,)), dma((len(UNITS),)), dma((1,)), dma((len(UNITS),)), dma((4,)), dma((4,)), dma((1,)), dma((len(UNITS),)),
         ],
         compiler_params=pltpu.CompilerParams(collective_id=0, has_side_effects=True, vmem_limit_bytes=60 * 1024 * 1024),
     )(raw_echoes, range_filter, azimuth_filter, inversion[:, 0, :].T, pair_mask, *[jnp.asarray(c) for c in consts])

time: 49.3 us -> 47.5 us (0.963)
  Pallas kernels: 48.5 us -> 46.7 us
    pallas_call x1, Pallas kernels: 48.5 us -> 46.7 us  [per_device(): pl.pallas_call(kernel, out_shape=pltpu.VMEM((1, 2, WIDE, 256), F32), in_s...]
where the time goes in v3:
time: 47.5 us; the launch traced here: 47.4 us
  Pallas kernels  46.7 us (98%)
  local copies, waits for them, and re-layouts  0.63 us (1%)
    pallas_call x1, Pallas kernels, per_device(): pl.pallas_call(kernel, out_shape=pltpu.VMEM((1, 2, WIDE, 256), F32), in_s...  46.7 us

profile of v3, /device:TPU:1, one launch (start us, length us, event | category | flops | bytes accessed | tf_op | source)
XLA Modules:
  0.0 47.4 jit_solution(13953283495652664077)
XLA Ops:
  0.0 46.7 %shard_map.127 = f32[1,2,32,256]{3,2,1,0:T(8,128)S(1)} custom-call(f32[1,2,64,2048]{3,2,1,0:T(8,128)} %raw.1, f32[2,2048]{1,0:T(2,128)} %rfil.1, f32[2,1024,128]{2,1,0:T(8,128)} %afil.1, f32[2,16]{1,0:T(2,128)} %bitcast.3, s32[1,2]{1,0:T(1,128)} %flags.1, bf16[768,256]{1,0:T(8,128)(2,1)} %constant.16.clone.w1_h, bf16[768,256]{1,0:T(8,128)(2,1)} %constant.17.clone.w2_h, ...), custom_call_target="tpu_custom_call" | custom-call | tf_op jit(solution)/shard_map/pallas_call | solution.py:609
  46.7 0.6 %copy.15 = f32[1,2,32,256]{3,2,1,0:T(8,128)} copy(f32[1,2,32,256]{3,2,1,0:T(8,128)S(1)} %shard_map.127) | data formatting | bytes 131072
